TPU v7x, 512 devices: a whole 4x8x8 slice. The times are simulated.
512 devices in a mesh: node: 64 (over y, z), col: 8 (over x, core).
Axes of the slice: x: 4, y: 8, z: 8, core: 2. Of those that a mesh axis runs over, the one named last changes fastest.
Arguments:
- x_t: bfloat16 [512, 32768], P('col', 'node'), may hold values from -6 to 6
- adj_tiles: bfloat16 [4096, 128, 128], P('node'), may hold values from -0.1875 to 0.1875
- tile_rows: int32 [4096], P('node'), may hold values from 0 to 3
- tile_cols: int32 [4096], P('node'), may hold values from 0 to 255, as said below
- tile_counts: int32 [64], P('node'), may hold values from 8 to 64, as said below
- w_first: bfloat16 [512, 512], P('col'), may hold values from -0.25 to 0.25
- b_first: float32 [512], P('col'), may hold values from -3 to 3
- w_second: bfloat16 [512, 512], P('col'), may hold values from -0.25 to 0.25
- b_second: float32 [512], P('col'), may hold values from -3 to 3
Outputs:
- out_t: float32 [512, 32768], P('col', 'node')
Inputs may be any that keep to these rules, and one draw needn't show every extreme that they name: `tile_cols`: column blocks q * 4 to q * 4 + 3 belong to device q of node. Among the live tiles of one device, at most 2 distinct column blocks belong to any one device, and every device's first 2 tiles name 2 distinct blocks of one device. `tile_counts`: some device has all 64 slots live.
All inputs are finite; a program needn't handle non-finite values.
Results may differ from a plain program's by a relative error of at most 0.004.
Values may be sent and summed in bfloat16 or wider, within the bound.
A program may use at most 64 MiB of HBM per device.

v0:
```python
import jax
import jax.numpy as jnp
from jax import lax
from jax.sharding import PartitionSpec as P

BLK = 128
CAP = 2


def tile_sum(x_blocks, tile_values, selector):
    products = jnp.einsum("fnj,nij->fni", x_blocks, tile_values, preferred_element_type=jnp.float32)
    return jnp.einsum("fni,nb->fbi", products, selector, precision=lax.Precision.HIGHEST)


def aggregate(feat_t, adj_tiles, tile_rows, live_count, plan):
    feat_local = feat_t.shape[0]
    row_blocks = feat_t.shape[1] // BLK
    tile_total = adj_tiles.shape[0]
    asked_of, tile_slot = plan
    own_blocks = feat_t.reshape(feat_local, row_blocks, BLK)
    outgoing = jnp.take(own_blocks, asked_of.reshape(-1), axis=1)
    incoming = lax.all_to_all(outgoing, "node", split_axis=1, concat_axis=1, tiled=True)
    x_blocks = jnp.take(incoming, tile_slot, axis=1)
    is_live = jnp.arange(tile_total, dtype=jnp.int32) < live_count
    selector = (
        (tile_rows[:, None] == jnp.arange(row_blocks, dtype=jnp.int32)[None, :]) & is_live[:, None]
    ).astype(jnp.float32)
    summed = tile_sum(x_blocks, adj_tiles, selector)
    return summed.reshape(feat_local, row_blocks * BLK).astype(jnp.bfloat16)


def dense_layer(aggregated, weight_local, bias_local):
    summed = jnp.dot(
        weight_local,
        lax.all_gather(aggregated, "col", axis=0, tiled=True),
        preferred_element_type=jnp.float32,
    )
    return summed + bias_local[:, None]


def body(x_t, adj_tiles, tile_rows, tile_cols, tile_counts, w_first, b_first, w_second, b_second):
    row_blocks = x_t.shape[1] // BLK
    peer_count = lax.axis_size("node")
    block_total = peer_count * row_blocks
    live_count = tile_counts[0]
    is_live = jnp.arange(tile_cols.shape[0], dtype=jnp.int32) < live_count
    named = (tile_cols[:, None] == jnp.arange(block_total, dtype=jnp.int32)[None, :]) & is_live[
        :, None
    ]
    needed = jnp.any(named, axis=0).astype(jnp.int32).reshape(peer_count, row_blocks)
    position = jnp.cumsum(needed, axis=1) - 1
    slot_hit = (needed[:, :, None] == 1) & (
        position[:, :, None] == jnp.arange(CAP, dtype=jnp.int32)[None, None, :]
    )
    wanted = jnp.sum(
        slot_hit.astype(jnp.int32) * jnp.arange(row_blocks, dtype=jnp.int32)[None, :, None], axis=1
    )
    asked_of = lax.all_to_all(wanted, "node", split_axis=0, concat_axis=0, tiled=True)
    owner_base = (jnp.arange(peer_count, dtype=jnp.int32) * CAP)[:, None]
    slot_table = (owner_base + jnp.clip(position, 0, CAP - 1)).reshape(-1)
    tile_slot = jnp.take(slot_table, tile_cols)
    plan = (asked_of, tile_slot)
    y_first = aggregate(x_t, adj_tiles, tile_rows, live_count, plan)
    h_first = jnp.maximum(dense_layer(y_first, w_first, b_first), 0.0).astype(jnp.bfloat16)
    y_second = aggregate(h_first, adj_tiles, tile_rows, live_count, plan)
    return dense_layer(y_second, w_second, b_second)


def solution(mesh):
    return jax.shard_map(
        body,
        mesh=mesh,
        in_specs=(
            P("col", "node"),
            P("node", None, None),
            P("node"),
            P("node"),
            P("node"),
            P("col", None),
            P("col"),
            P("col", None),
            P("col"),
        ),
        out_specs=P("col", "node"),
        check_vma=False,
    )
```

profile of v0, /device:TPU:25, one launch (start us, length us, event | category | flops | bytes accessed | tf_op | source)
XLA Modules:
  0.0 206.9 jit_solution(1067784979185888805)
XLA Ops:
  0.0 0.0 copy-start
  0.8 0.8 fusion.23
  1.6 0.1 reshape.72
  1.7 0.1 copy.23
  1.8 0.2 reduce_window_sum.11
  2.0 0.1 clamp_add_fusion
  2.1 0.1 copy.24
  2.2 0.7 copy.25
  2.9 15.8 %all-to-all-start = ((s32[64,1,2]{2,1,0:T(1,128)}), s32[64,1,2]{2,1,0:T(1,128)S(1)}, u32[]{:S(2)}, u32[]{:S(2)}) async-start(s32[64,1,2]{2,1,0:T(1,128)} %copy.25), calls=%async_computation | async-start | bytes 65536 | tf_op jit(solution)/shard_map/all_to_all | solution.py:58
  18.7 0.9 copy_bitcast_fusion.3
  19.6 7.5 %all-to-all-done = s32[64,1,2]{2,1,0:T(1,128)S(1)} async-done(((s32[64,1,2]{2,1,0:T(1,128)}), s32[64,1,2]{2,1,0:T(1,128)S(1)}, u32[]{:S(2)}, u32[]{:S(2)}) %all-to-all-start) | async-done | bytes 544 | tf_op jit(solution)/shard_map/all_to_all | solution.py:58
  27.1 0.5 broadcast.114
  27.6 0.7 reduce.3
  28.3 0.1 reshape.70
  28.5 2.1 %gather_fusion.1 = bf16[128,64,128]{2,1,0:T(8,128)(2,1)} fusion(bf16[64,4,128]{2,0,1:T(8,128)(2,1)S(1)} %copy_bitcast_fusion.3, s32[1024]{0:T(1024)S(1)} %pad_clamp_fusion.1), kind=kCustom, calls=%fused_computation.clone | custom fusion | bytes 4194816 | tf_op jit(solution)/shard_map/jit(_take)/gather | solution.py:21
  30.6 3.2 %select_bitcast_fusion.1 = bf16[64,128,128]{2,0,1:T(8,128)(2,1)} fusion(bf16[128,64,128]{2,1,0:T(8,128)(2,1)} %gather_fusion.1, pred[128]{0:T(512)(128)(4,1)S(1)} %compare_and_fusion.1), kind=kLoop, calls=%fused_computation.10 | loop fusion | flops 1048576 | bytes 4194432 | tf_op jit(solution)/shard_map/jit(_take)/select_n | solution.py:21
  33.8 0.0 copy-start.5
  33.8 8.0 %all-to-all-start.1 = ((bf16[64,128,128]{2,0,1:T(8,128)(2,1)}), bf16[64,128,128]{2,0,1:T(8,128)(2,1)}, u32[]{:S(2)}, u32[]{:S(2)}) async-start(bf16[64,128,128]{2,0,1:T(8,128)(2,1)} %select_bitcast_fusion.1), calls=%async_computation.1 | async-start | bytes 4194304 | tf_op jit(solution)/shard_map/all_to_all | solution.py:22
  41.8 0.1 add.63
  41.9 0.0 copy-done.5
  42.0 0.8 gather_fusion
  42.8 53.7 %all-to-all-done.1 = bf16[64,128,128]{2,0,1:T(8,128)(2,1)} async-done(((bf16[64,128,128]{2,0,1:T(8,128)(2,1)}), bf16[64,128,128]{2,0,1:T(8,128)(2,1)}, u32[]{:S(2)}, u32[]{:S(2)}) %all-to-all-start.1) | async-done | bytes 2097184 | tf_op jit(solution)/shard_map/all_to_all | solution.py:22
  96.5 2.3 %gather_fusion.2 = bf16[64,64,128]{2,1,0:T(8,128)(2,1)S(1)} fusion(bf16[64,128,128]{2,0,1:T(8,128)(2,1)} %all-to-all-done.1, s32[1024]{0:T(1024)S(1)} %pad_clamp_fusion), kind=kCustom, calls=%fused_computation.1.clone | custom fusion | bytes 2097408 | tf_op jit(solution)/shard_map/jit(_take)/gather | solution.py:23
  98.8 0.0 copy-done
  98.8 0.0 copy-start.3
  98.8 1.5 convolution_bitcast_fusion.1
  100.4 0.0 copy-done.3
  100.4 0.0 copy-start.1
  100.4 0.0 copy-start.6
  100.4 2.0 fusion.7
  102.4 15.1 %all_gather.6 = bf16[512,512]{1,0:T(8,128)(2,1)S(1)} all-gather(bf16[64,512]{1,0:T(8,128)(2,1)S(1)} %bitcast.53), channel_id=1, replica_groups=mesh['node'=64,'col'=8] {'col'}, dimensions={0}, use_global_device_ids=true | all-gather | bytes 589824 | tf_op jit(solution)/shard_map/all_gather | solution.py:35
  117.5 0.0 copy-done.1
  117.5 0.0 copy-done.6
  117.5 0.2 fusion.13
  117.7 2.2 %gather_fusion.3 = bf16[128,64,128]{2,1,0:T(8,128)(2,1)} fusion(bf16[64,4,128]{2,0,1:T(8,128)(2,1)S(1)} %bitcast.50, s32[1024]{0:T(1024)S(1)} %pad_clamp_fusion.1), kind=kCustom, calls=%fused_computation.2.clone | custom fusion | bytes 4194816 | tf_op jit(solution)/shard_map/jit(_take)/gather | solution.py:21
  119.9 1.9 select_bitcast_fusion
  121.7 62.4 %all_to_all.19 = bf16[64,128,128]{2,0,1:T(8,128)(2,1)} all-to-all(bf16[64,128,128]{2,0,1:T(8,128)(2,1)S(1)} %select_bitcast_fusion), channel_id=1, replica_groups=mesh['node'=64,'col'=8] {'node'}, dimensions={1} | all-to-all | bytes 4194304 | tf_op jit(solution)/shard_map/all_to_all | solution.py:22
  184.1 2.3 %gather_fusion.4 = bf16[64,64,128]{2,1,0:T(8,128)(2,1)S(1)} fusion(bf16[64,128,128]{2,0,1:T(8,128)(2,1)} %all_to_all.19, s32[1024]{0:T(1024)S(1)} %pad_clamp_fusion), kind=kCustom, calls=%fused_computation.3.clone | custom fusion | bytes 2097408 | tf_op jit(solution)/shard_map/jit(_take)/gather | solution.py:23
  186.4 1.5 convolution_bitcast_fusion
  188.0 0.0 copy-start.2
  188.0 0.0 copy-start.4
  188.0 2.0 fusion.10
  190.0 16.0 %all_gather.7 = bf16[512,512]{1,0:T(8,128)(2,1)S(1)} all-gather(bf16[64,512]{1,0:T(8,128)(2,1)S(1)} %bitcast.54), channel_id=1, replica_groups=mesh['node'=64,'col'=8] {'col'}, dimensions={0}, use_global_device_ids=true | all-gather | bytes 589824 | tf_op jit(solution)/shard_map/all_gather | solution.py:35
  206.0 0.0 copy-done.2
  206.0 0.0 copy-done.4
  206.0 0.9 fusion.4
  (15 shorter events, 0.1 us)
Async XLA Ops:
  0.0 98.8 %copy-start = (bf16[64,128,128]{2,1,0:T(8,128)(2,1)S(1)}, bf16[64,128,128]{2,1,0:T(8,128)(2,1)}, u32[]{:S(2)}) copy-start(bf16[64,128,128]{2,1,0:T(8,128)(2,1)} %param.14) | copy-start | bytes 6291460
  2.9 24.2 %all-to-all-start = ((s32[64,1,2]{2,1,0:T(1,128)}), s32[64,1,2]{2,1,0:T(1,128)S(1)}, u32[]{:S(2)}, u32[]{:S(2)}) async-start(s32[64,1,2]{2,1,0:T(1,128)} %copy.25), calls=%async_computation | async-start | bytes 65536 | tf_op jit(solution)/shard_map/all_to_all | solution.py:58
  33.8 8.1 %copy-start.5 = (s32[64]{0:T(128)S(1)}, s32[64]{0:T(128)}, u32[]{:S(2)}) copy-start(s32[64]{0:T(128)} %param.16) | copy-start | bytes 772
  33.8 62.7 %all-to-all-start.1 = ((bf16[64,128,128]{2,0,1:T(8,128)(2,1)}), bf16[64,128,128]{2,0,1:T(8,128)(2,1)}, u32[]{:S(2)}, u32[]{:S(2)}) async-start(bf16[64,128,128]{2,0,1:T(8,128)(2,1)} %select_bitcast_fusion.1), calls=%async_computation.1 | async-start | bytes 4194304 | tf_op jit(solution)/shard_map/all_to_all | solution.py:22
  98.8 1.6 copy-start.3
  100.4 17.1 %copy-start.1 = (bf16[64,512]{1,0:T(8,128)(2,1)S(1)}, bf16[64,512]{1,0:T(8,128)(2,1)}, u32[]{:S(2)}) copy-start(bf16[64,512]{1,0:T(8,128)(2,1)} %param.18) | copy-start | bytes 196612
  100.4 17.1 %copy-start.6 = (f32[64]{0:T(128)S(1)}, f32[64]{0:T(128)}, u32[]{:S(2)}) copy-start(f32[64]{0:T(128)} %param.19) | copy-start | bytes 772
  188.0 18.1 %copy-start.2 = (bf16[64,512]{1,0:T(8,128)(2,1)S(1)}, bf16[64,512]{1,0:T(8,128)(2,1)}, u32[]{:S(2)}) copy-start(bf16[64,512]{1,0:T(8,128)(2,1)} %param.20) | copy-start | bytes 196612
  188.0 18.0 %copy-start.4 = (f32[64]{0:T(128)S(1)}, f32[64]{0:T(128)}, u32[]{:S(2)}) copy-start(f32[64]{0:T(128)} %param.21) | copy-start | bytes 772
where the time goes:
time: 207 us
  blocking collectives  93.5 us (45%)
  waiting for transfers between devices  61.2 us (30%)
  starting transfers between devices  23.9 us (12%)
  local copies, waits for them, and re-layouts  12.4 us (6%)
  matrix products  8.07 us (4%)
  other arithmetic  6.84 us (3%)
    all_to_all x1, blocking collectives, aggregate(): lax.all_to_all(outgoing, 'node', split_axis=1, concat_axis=1, tiled=True)  62.4 us
    all_to_all x1, waiting for transfers between devices, aggregate(): lax.all_to_all(outgoing, 'node', split_axis=1, concat_axis=1, tiled=True)  53.7 us
    all_gather x2, blocking collectives, dense_layer(): lax.all_gather(aggregated, 'col', axis=0, tiled=True)  31.1 us
    all_to_all x1, starting transfers between devices, body(): lax.all_to_all(wanted, 'node', split_axis=0, concat_axis=0, tiled=True)  15.8 us
    all_to_all x1, starting transfers between devices, aggregate(): lax.all_to_all(outgoing, 'node', split_axis=1, concat_axis=1, tiled=True)  8.02 us
    all_to_all x1, waiting for transfers between devices, body(): lax.all_to_all(wanted, 'node', split_axis=0, concat_axis=0, tiled=True)  7.51 us
    select_n x3, other arithmetic, aggregate(): outgoing = jnp.take(own_blocks, asked_of.reshape(-1), axis=1)  5.01 us
    gather x2, local copies, waits for them, and re-layouts, aggregate(): x_blocks = jnp.take(incoming, tile_slot, axis=1)  4.68 us
  transfers between devices with their start and end apart: 2, of which 2 were waited for; matrix products, arithmetic and copies ran while one was open for 1% of the time, Pallas kernels for 0%

commit v1 on v0

v1 whole, which is shorter than its diff:
```python
import jax
import jax.numpy as jnp
from jax import lax
from jax.experimental import pallas as pl
from jax.experimental.pallas import tpu as pltpu
from jax.sharding import PartitionSpec as P

BLK = 128
RB = 4
GROUP = 8


def tile_sum(index_ref, rows_ref, live, gathered, tiles):
    feat = gathered.shape[1]
    total = tiles.shape[0]

    def step(g, acc):
        left, right = [], []
        for k in range(GROUP):
            t = g * GROUP + k
            block = gathered[index_ref[t]]
            row = jnp.where(t < live, rows_ref[t], RB)
            zero = jnp.zeros_like(block)
            left.append(jnp.concatenate([jnp.where(row == b, block, zero) for b in range(RB)], axis=0))
            right.append(tiles[t])
        return acc + lax.dot_general(
            jnp.concatenate(left, axis=1),
            jnp.concatenate(right, axis=1),
            (((1,), (1,)), ((), ())),
            preferred_element_type=jnp.float32,
        )

    return lax.fori_loop(0, total // GROUP, step, jnp.zeros((RB * feat, BLK), jnp.float32))


def agg_kernel(cols_ref, rows_ref, count_ref, g_ref, tiles_ref, bias_ref, out_ref):
    feat = g_ref.shape[1]
    acc = tile_sum(cols_ref, rows_ref, count_ref[0], g_ref, tiles_ref)
    for b in range(RB):
        out_ref[:, b * BLK : (b + 1) * BLK] = (acc[b * feat : (b + 1) * feat] + bias_ref[...]).astype(out_ref.dtype)


def aggregate(blocks, tiles, cols, rows, count, bias, dtype):
    feat = blocks.shape[1]
    gathered = lax.all_gather(blocks, "node", axis=0, tiled=True)
    smem = pl.BlockSpec(memory_space=pltpu.SMEM)
    vmem = pl.BlockSpec(memory_space=pltpu.VMEM)
    return pl.pallas_call(
        agg_kernel,
        out_shape=jax.ShapeDtypeStruct((feat, RB * BLK), dtype),
        in_specs=[smem, smem, smem, vmem, vmem, vmem],
        out_specs=vmem,
    )(cols, rows, count, gathered, tiles, bias)


def to_blocks(feat_t):
    feat = feat_t.shape[0]
    return jnp.transpose(feat_t.reshape(feat, RB, BLK), (1, 0, 2))


def body(x_t, adj_tiles, tile_rows, tile_cols, tile_counts, w_first, b_first, w_second, b_second):
    feat = x_t.shape[0]
    w_all = lax.all_gather(w_first, "col", axis=0, tiled=True)
    b_all = lax.all_gather(b_first, "col", axis=0, tiled=True)
    none = jnp.zeros((feat, 1), jnp.float32)
    y_first = aggregate(to_blocks(x_t), adj_tiles, tile_cols, tile_rows, tile_counts, none, jnp.bfloat16)
    y_all = lax.all_gather(y_first, "col", axis=0, tiled=True)
    z_first = jnp.dot(w_all, y_all, preferred_element_type=jnp.float32) + b_all[:, None]
    h_first = jnp.maximum(z_first, 0.0).astype(jnp.bfloat16)
    z_second = jnp.dot(w_second, h_first, preferred_element_type=jnp.float32).astype(jnp.bfloat16)
    return aggregate(to_blocks(z_second), adj_tiles, tile_cols, tile_rows, tile_counts, b_second[:, None], jnp.float32)


def solution(mesh):
    return jax.shard_map(
        body,
        mesh=mesh,
        in_specs=(
            P("col", "node"),
            P("node", None, None),
            P("node"),
            P("node"),
            P("node"),
            P("col", None),
            P("col"),
            P("col", None),
            P("col"),
        ),
        out_specs=P("col", "node"),
        check_vma=False,
    )
```

time: 207 us -> 220 us (1.063)
  the two profiles are of different devices: /device:TPU:25 before, /device:TPU:2 now
where the time goes in v1:
time: 220 us
  waiting for transfers between devices  145 us (66%)
  blocking collectives  41.9 us (19%)
  between operations  14.7 us (7%)
  Pallas kernels  12 us (5%)
  local copies, waits for them, and re-layouts  5.66 us (3%)
    all_gather x2, waiting for transfers between devices, aggregate(): gathered = lax.all_gather(blocks, 'node', axis=0, tiled=True)  145 us
    unnamed x1, blocking collectives  14.8 us
    all_gather x1, blocking collectives, body(): w_all = lax.all_gather(w_first, 'col', axis=0, tiled=True)  13.7 us
    all_gather x1, blocking collectives, body(): y_all = lax.all_gather(y_first, 'col', axis=0, tiled=True)  13.3 us
    pallas_call x2, Pallas kernels, aggregate(): pl.pallas_call(agg_kernel, out_shape=jax.ShapeDtypeStruct((feat, RB * BLK...  12 us
  transfers between devices with their start and end apart: 2, of which 2 were waited for; matrix products, arithmetic and copies ran while one was open for 1% of the time, Pallas kernels for 0%

profile of v1, /device:TPU:2, one launch (start us, length us, event | category | flops | bytes accessed | tf_op | source)
XLA Modules:
  0.0 220.1 jit_solution(10829102648900193217)
XLA Ops:
  6.5 0.0 copy-start
  6.5 0.0 all-gather.3.cloned.1.call-start
  6.5 0.9 reshape.7
  7.4 0.6 copy.14
  8.1 0.0 all-gather.3.cloned.1.call-update
  8.1 0.0 all-gather.5.cloned.1.call-start
  8.8 1.3 dynamic-slice
  10.7 0.9 dynamic-update-slice
  11.6 14.8 %all-reduce = f32[512]{0:T(512)S(1)} all-reduce(f32[512]{0:T(512)S(1)} %dynamic-update-slice), channel_id=1, replica_groups=mesh['node'=64,'col'=8] {'col'}, use_global_device_ids=true, to_apply=%add | all-reduce | flops 512 | bytes 4096
  26.4 13.7 %all_gather.17 = bf16[512,512]{1,0:T(8,128)(2,1)S(1)} all-gather(bf16[64,512]{1,0:T(8,128)(2,1)} %param.14), channel_id=1, replica_groups=mesh['node'=64,'col'=8] {'col'}, dimensions={0}, use_global_device_ids=true | all-gather | bytes 589824 | tf_op jit(solution)/shard_map/all_gather | solution.py:63
  40.1 62.0 %all-gather.3.cloned.1.call-done.g_ref = bf16[256,64,128]{2,1,0:T(8,128)(2,1)} async-done(((bf16[4,64,128]{2,1,0:T(8,128)(2,1)}), bf16[256,64,128]{2,1,0:T(8,128)(2,1)}) %all-gather.3.cloned.1.call-update) | async-done | bytes 4194320 | tf_op jit(solution)/shard_map/all_gather | solution.py:45
  102.2 0.6 broadcast_in_dim.7.bias_ref
  102.8 0.0 copy-start.1
  102.8 6.0 %shard_map.91 = bf16[64,512]{1,0:T(8,128)(2,1)} custom-call(s32[64]{0:T(128)} %cols_ref.3, s32[64]{0:T(128)} %rows_ref.3, s32[1]{0:T(128)S(6)} %copy.18.count_ref, bf16[256,64,128]{2,1,0:T(8,128)(2,1)} %all-gather.3.cloned.1.call-done.g_ref, bf16[64,128,128]{2,1,0:T(8,128)(2,1)} %tiles_ref.3, f32[64,1]{1,0:T(8,128)} %broadcast_in_dim.7.bias_ref), custom_call_target="tpu_custom_call" | custom-call | tf_op jit(solution)/shard_map/pallas_call | solution.py:48
  108.8 13.3 %all_gather.16 = bf16[512,512]{1,0:T(8,128)(2,1)S(1)} all-gather(bf16[64,512]{1,0:T(8,128)(2,1)} %shard_map.91), channel_id=1, replica_groups=mesh['node'=64,'col'=8] {'col'}, dimensions={0}, use_global_device_ids=true | all-gather | bytes 589824 | tf_op jit(solution)/shard_map/all_gather | solution.py:67
  122.1 0.0 copy-done
  122.1 0.7 fusion.4
  122.8 0.6 copy.15
  123.5 0.0 all-gather.5.cloned.1.call-update
  123.5 0.0 copy-done.1
  123.5 0.7 copy.16.bias_ref
  124.2 83.0 %all-gather.5.cloned.1.call-done.g_ref = bf16[256,64,128]{2,1,0:T(8,128)(2,1)} async-done(((bf16[4,64,128]{2,1,0:T(8,128)(2,1)}), bf16[256,64,128]{2,1,0:T(8,128)(2,1)}) %all-gather.5.cloned.1.call-update) | async-done | bytes 4194320 | tf_op jit(solution)/shard_map/all_gather | solution.py:45
  207.2 6.0 %shard_map.92 = f32[64,512]{1,0:T(8,128)} custom-call(s32[64]{0:T(128)} %cols_ref.3, s32[64]{0:T(128)} %rows_ref.3, s32[1]{0:T(128)S(6)} %copy.18.count_ref, bf16[256,64,128]{2,1,0:T(8,128)(2,1)} %all-gather.5.cloned.1.call-done.g_ref, bf16[64,128,128]{2,1,0:T(8,128)(2,1)} %tiles_ref.3, f32[64,1]{1,0:T(8,128)} %copy.16.bias_ref), custom_call_target="tpu_custom_call" | custom-call | tf_op jit(solution)/shard_map/pallas_call | solution.py:48
  (2 shorter events, 0.0 us)
Async XLA Ops:
  6.5 115.6 %copy-start = (bf16[64,512]{1,0:T(8,128)(2,1)S(1)}, bf16[64,512]{1,0:T(8,128)(2,1)}, u32[]{:S(2)}) copy-start(bf16[64,512]{1,0:T(8,128)(2,1)} %param.16) | copy-start | bytes 196612
  6.5 95.6 %all-gather.3.cloned.1.call-start = ((), (), s32[]{:S(2)}) async-start(), calls=%async_computation | async-start | bytes 4259840 | tf_op jit(solution)/shard_map/all_gather | solution.py:45
  8.1 199.1 %all-gather.5.cloned.1.call-start = ((), (), s32[]{:S(2)}) async-start(), calls=%async_computation.1 | async-start | bytes 4259840 | tf_op jit(solution)/shard_map/all_gather | solution.py:45
  102.8 20.7 %copy-start.1 = (f32[64]{0:T(128)S(1)}, f32[64]{0:T(128)}, u32[]{:S(2)}) copy-start(f32[64]{0:T(128)} %param.17) | copy-start | bytes 772
Sparse Core Ops, SparseCore 0:
  10.4 91.7 all-gather.2
  123.6 83.5 all-gather.4

commit v2 on v1

v2 whole, which is shorter than its diff:
```python
import heapq
import itertools

import jax
import jax.numpy as jnp
from jax import lax
from jax.experimental import pallas as pl
from jax.experimental.pallas import tpu as pltpu
from jax.sharding import PartitionSpec as P

MESH = pl.DeviceIdType.MESH
BLK = 128
RB = 4
GROUP = 8
SIDE = 8
FAR, NEAR = 4, 3
HALF = 2
SLOTS = 64


def children(flow, at):
    first, second = (0, 1) if flow == 0 else (1, 0)
    out = []

    def step(axis):
        here = at[axis]
        for sign in (1, -1):
            if (sign > 0 and 0 <= here < FAR) or (sign < 0 and -NEAR < here <= 0):
                there = list(at)
                there[axis] += sign
                out.append((tuple(there), axis, sign))

    if at[second] == 0:
        step(first)
    step(second)
    return out


def depth(flow, at):
    return max([1 + depth(flow, there) for there, _, _ in children(flow, at)], default=0)


def arrival_order():
    wire, hop = 0.7, 1.7
    free = {}
    tick = itertools.count()
    events = [(0.0, next(tick), flow, (0, 0)) for flow in (0, 1)]
    order = []
    while events:
        now, _, flow, at = heapq.heappop(events)
        order.append((flow, at))
        for there, axis, sign in sorted(children(flow, at), key=lambda c: -depth(flow, c[0])):
            start = max(now, free.get((axis, sign), 0.0))
            free[(axis, sign)] = start + wire
            heapq.heappush(events, (free[(axis, sign)] + hop, next(tick), flow, there))
    return order


def slot_of(at):
    return (at[0] + NEAR) * SIDE + at[1] + NEAR


class Place:
    def __init__(self):
        self.node, self.col = lax.axis_index("node"), lax.axis_index("col")
        self.y, self.z = self.node // SIDE, self.node % SIDE
        self.x, self.core = self.col // 2, self.col % 2
        self.sign = 1 - 2 * self.core
        self.ys = {a: (self.y - self.sign * a + 2 * SIDE) % SIDE for a in range(-NEAR, FAR + 1)}
        self.zs = {a: (self.z - self.sign * a + 2 * SIDE) % SIDE for a in range(-NEAR, FAR + 1)}

    def source(self, at):
        return self.ys[at[0]] * SIDE + self.zs[at[1]]

    def toward(self, axis, sign):
        y, z = (self.ys[-sign], self.z) if axis == 0 else (self.y, self.zs[-sign])
        return (y * SIDE + z, self.col)

    def beside(self, dx, other):
        core = 1 - self.core if other else self.core
        return (self.node, (self.x + dx) % 4 * 2 + core)


def remote(src, dst, send, recv, device):
    return pltpu.make_async_remote_copy(
        src_ref=src, dst_ref=dst, send_sem=send, recv_sem=recv, device_id=device, device_id_type=MESH
    )


def node_gather(place, held, send, recv, ends, own, between=None):
    here = (place.node, place.col)
    last = 0
    for count, (flow, at) in enumerate(arrival_order()):
        rows = held.at[pl.ds(place.source(at) * RB + flow * HALF, HALF)]
        onward = sorted(children(flow, at), key=lambda c: -depth(flow, c[0]))
        if at != (0, 0):
            if not onward:
                last += 1
                continue
            remote(rows, rows, send, recv.at[flow * SLOTS + slot_of(at)], here).wait_recv()
        for there, axis, sign in onward:
            ending = not children(flow, there)
            sem = ends if ending else recv.at[flow * SLOTS + slot_of(there)]
            device = place.toward(axis, sign)
            if at == (0, 0) and own is not None:
                for k in range(flow * HALF, flow * HALF + HALF):
                    remote(own(k), held.at[place.node * RB + k], send, sem, device).start()
            else:
                remote(rows, rows, send, sem, device).start()
        if between is not None:
            between(count)
    whole = held.at[pl.ds(0, last * HALF)]
    remote(whole, whole, send, ends, here).wait_recv()
    sent = held.at[pl.ds(0, (SIDE * SIDE - 1) * RB)]
    remote(sent, sent, send, ends, here).wait_send()


class ColGather:
    def __init__(self, place, own, rows, feat, send, recv):
        self.place, self.own, self.rows, self.feat, self.send, self.recv = place, own, rows, feat, send, recv
        self.half = feat // 2

    def cut(self, x, core, part):
        start = (x % 4 * 2 + core) * self.feat
        if part is None:
            return self.rows.at[pl.ds(start, self.feat)]
        return self.rows.at[pl.ds(start + part * self.half, self.half)]

    def mine(self, part):
        if part is None:
            return self.own
        return self.own.at[pl.ds(part * self.half, self.half)]

    def begin(self):
        p = self.place
        for dx, part, sem in ((1, 0, 0), (-1, 1, 3), (1, 1, 1), (-1, 0, 2)):
            remote(self.mine(part), self.cut(p.x, p.core, part), self.send, self.recv.at[sem], p.beside(dx + 4, False)).start()
        remote(self.mine(None), self.cut(p.x, p.core, None), self.send, self.recv.at[4], p.beside(0, True)).start()

    def wait(self, dx, other, part, sem):
        p = self.place
        core = 1 - p.core if other else p.core
        rows = self.cut(p.x + dx + 4, core, part)
        remote(rows, rows, self.send, self.recv.at[sem], (p.node, p.col)).wait_recv()
        return rows

    def forward(self, stage):
        p = self.place
        if stage == 0:
            for dx, part, sem, on, far in ((-1, 0, 0, 1, 5), (1, 1, 3, -1, 6), (-1, 1, 1, 0, 0), (1, 0, 2, 0, 0)):
                rows = self.wait(dx, False, part, sem)
                if on:
                    remote(rows, rows, self.send, self.recv.at[far], p.beside(on + 4, False)).start()
                remote(rows, rows, self.send, self.recv.at[7 + sem], p.beside(0, True)).start()
        else:
            for part, sem in ((0, 5), (1, 6)):
                rows = self.wait(2, False, part, sem)
                remote(rows, rows, self.send, self.recv.at[6 + sem], p.beside(0, True)).start()

    def finish(self):
        self.wait(0, True, None, 4)
        for dx, part, sem in ((-1, 0, 7), (-1, 1, 8), (1, 0, 9), (1, 1, 10), (2, 0, 11), (2, 1, 12)):
            self.wait(dx, True, part, sem)
        sent = self.rows.at[pl.ds(0, 7 * self.feat)]
        remote(sent, sent, self.send, self.recv.at[0], (self.place.node, self.place.col)).wait_send()


def tile_sum(index_ref, rows_ref, live, gathered, tiles):
    feat = gathered.shape[1]
    total = tiles.shape[0]

    def step(g, acc):
        left, right = [], []
        for k in range(GROUP):
            t = g * GROUP + k
            block = gathered[index_ref[t]]
            row = jnp.where(t < live, rows_ref[t], RB)
            zero = jnp.zeros_like(block)
            left.append(jnp.concatenate([jnp.where(row == b, block, zero) for b in range(RB)], axis=0))
            right.append(tiles[t])
        return acc + lax.dot_general(
            jnp.concatenate(left, axis=1),
            jnp.concatenate(right, axis=1),
            (((1,), (1,)), ((), ())),
            preferred_element_type=jnp.float32,
        )

    return lax.fori_loop(0, total // GROUP, step, jnp.zeros((RB * feat, BLK), jnp.float32))


def as_column(row):
    size = row.shape[1]
    square = jnp.broadcast_to(row, (size, size))
    same = lax.broadcasted_iota(jnp.int32, (size, size), 0) == lax.broadcasted_iota(jnp.int32, (size, size), 1)
    return jnp.sum(jnp.where(same, square, 0.0), axis=1, keepdims=True)


def kernel(
    cols_ref, rows_ref, count_ref, x_ref, adj_ref, w1_ref, b1_ref, w2_ref, b2_ref, out_ref,
    held1, held2, tiles, w1_all, w2, b1_own, b1_all, y_own, y_all,
    recv1, recv2, col_recv, bias_recv, sends, local,
):
    feat = y_own.shape[0]
    place = Place()
    fetch = [
        pltpu.make_async_copy(adj_ref, tiles, local.at[0]),
        pltpu.make_async_copy(w2_ref, w2, local.at[1]),
        pltpu.make_async_copy(w1_ref, w1_all.at[pl.ds(place.col * feat, feat)], local.at[2]),
    ]
    for k in range(RB):
        fetch.append(pltpu.make_async_copy(x_ref.at[:, pl.ds(k * BLK, BLK)], held1.at[place.node * RB + k], local.at[3 + k]))
    for copy in fetch:
        copy.start()

    b1_own[...] = jnp.broadcast_to(as_column(b1_ref[...]), b1_own.shape)
    b1_all[pl.ds(place.col * feat, feat)] = b1_own[...]

    barrier = pltpu.get_barrier_semaphore()
    greeted = [place.toward(axis, sign) for axis in (0, 1) for sign in (1, -1)]
    greeted += [place.beside(dx, other) for dx in range(4) for other in (False, True) if dx or other]
    for device in greeted:
        pl.semaphore_signal(barrier, inc=1, device_id=device, device_id_type=MESH)
    pl.semaphore_wait(barrier, len(greeted))

    weights = ColGather(place, w1_ref, w1_all, feat, sends.at[2], col_recv.at[0])
    peers = [(dx, other) for dx in range(4) for other in (False, True) if dx or other]

    def bias_copy(index, dx, other, coming):
        core = 1 - place.core if other else place.core
        x = (place.x - dx + 4) % 4 if coming else place.x
        source = x * 2 + (core if coming else place.core)
        rows = b1_all.at[pl.ds(source * feat, feat)]
        return remote(b1_own, rows, sends.at[4], bias_recv.at[index], place.beside(dx, other))

    def between(count):
        if count == 1:
            weights.begin()
            for index, (dx, other) in enumerate(peers):
                bias_copy(index, dx, other, False).start()
        elif count == 20:
            weights.forward(0)
        elif count == 40:
            weights.forward(1)

    node_gather(place, held1, sends.at[0], recv1, recv1.at[2 * SLOTS], lambda k: x_ref.at[:, pl.ds(k * BLK, BLK)], between)
    weights.finish()
    for index, (dx, other) in enumerate(peers):
        bias_copy(index, dx, other, True).wait_recv()
    sent = b1_all.at[pl.ds(0, len(peers) * feat)]
    remote(sent, sent, sends.at[4], bias_recv.at[0], (place.node, place.col)).wait_send()
    for copy in fetch:
        copy.wait()

    live = count_ref[0]
    acc = tile_sum(cols_ref, rows_ref, live, held1, tiles)
    for b in range(RB):
        y_own[:, b * BLK : (b + 1) * BLK] = acc[b * feat : (b + 1) * feat].astype(y_own.dtype)
    y_all[pl.ds(place.col * feat, feat)] = y_own[...]
    exchange = ColGather(place, y_own, y_all, feat, sends.at[3], col_recv.at[1])
    exchange.begin()
    exchange.forward(0)
    exchange.forward(1)
    exchange.finish()

    wide = HALF * BLK
    step_rows = 128
    for n in range(RB // HALF):
        columns = pl.ds(n * wide, wide)
        total = jnp.zeros((feat, wide), jnp.float32)
        for m in range(w1_all.shape[0] // step_rows):
            span = pl.ds(m * step_rows, step_rows)
            z = jnp.dot(w1_all[span, :], y_all[:, columns], preferred_element_type=jnp.float32)
            bias = b1_all[span, :]
            h = jnp.maximum(z + jnp.concatenate([bias] * HALF, axis=1), 0.0).astype(jnp.bfloat16)
            total += jnp.dot(w2[:, span], h, preferred_element_type=jnp.float32)
        for k in range(HALF):
            held2[place.node * RB + n * HALF + k] = total[:, k * BLK : (k + 1) * BLK].astype(jnp.bfloat16)

    node_gather(place, held2, sends.at[1], recv2, recv2.at[2 * SLOTS], None)
    acc = tile_sum(cols_ref, rows_ref, live, held2, tiles)
    bias = as_column(b2_ref[...])
    for b in range(RB):
        out_ref[:, b * BLK : (b + 1) * BLK] = acc[b * feat : (b + 1) * feat] + bias


def body(x_t, adj_tiles, tile_rows, tile_cols, tile_counts, w_first, b_first, w_second, b_second):
    feat, nodes = x_t.shape
    channels = w_first.shape[1]
    blocks = SIDE * SIDE * RB
    smem = pl.BlockSpec(memory_space=pltpu.SMEM)
    vmem = pl.BlockSpec(memory_space=pltpu.VMEM)
    hbm = pl.BlockSpec(memory_space=pl.ANY)
    dma = pltpu.SemaphoreType.DMA
    bf16 = jnp.bfloat16
    return pl.pallas_call(
        kernel,
        out_shape=jax.ShapeDtypeStruct((feat, nodes), jnp.float32),
        in_specs=[smem, smem, smem, hbm, hbm, hbm, vmem, hbm, vmem],
        out_specs=vmem,
        scratch_shapes=[
            pltpu.VMEM((blocks, feat, BLK), bf16),
            pltpu.VMEM((blocks, feat, BLK), bf16),
            pltpu.VMEM(adj_tiles.shape, bf16),
            pltpu.VMEM((channels, channels), bf16),
            pltpu.VMEM((feat, channels), bf16),
            pltpu.VMEM((feat, BLK), jnp.float32),
            pltpu.VMEM((channels, BLK), jnp.float32),
            pltpu.VMEM((feat, nodes), bf16),
            pltpu.VMEM((channels, nodes), bf16),
            dma((2 * SLOTS + 1,)),
            dma((2 * SLOTS + 1,)),
            dma((2, 13)),
            dma((7,)),
            dma((5,)),
            dma((7,)),
        ],
        compiler_params=pltpu.CompilerParams(collective_id=0, has_side_effects=True),
    )(tile_cols, tile_rows, tile_counts, x_t, adj_tiles, w_first, b_first[None, :], w_second, b_second[None, :])


def solution(mesh):
    return jax.shard_map(
        body,
        mesh=mesh,
        in_specs=(
            P("col", "node"),
            P("node", None, None),
            P("node"),
            P("node"),
            P("node"),
            P("col", None),
            P("col"),
            P("col", None),
            P("col"),
        ),
        out_specs=P("col", "node"),
        check_vma=False,
    )
```

time: 220 us -> 103 us (0.47)
  waiting for transfers between devices: 145 us -> 0 us
  Pallas kernels: 12 us -> 101 us
  blocking collectives: 41.9 us -> 0 us
  between operations: 14.7 us -> 0.66 us
  local copies, waits for them, and re-layouts: 5.66 us -> 1.57 us
    all_gather x2 -> x0, waiting for transfers between devices: 145 us -> none  [aggregate(): gathered = lax.all_gather(blocks, 'node', axis=0, tiled=True)]
    pallas_call x2 -> x1, Pallas kernels: 12 us -> 101 us  [body(): pl.pallas_call(kernel, out_shape=jax.ShapeDtypeStruct((feat, nodes), jnp....]
    all_gather x2 -> x0, blocking collectives: 27 us -> none  [the longest x1 13.7 us: body(): w_all = lax.all_gather(w_first, 'col', axis=0, tiled=True)]
    unnamed x1 -> x0, blocking collectives: 14.8 us -> none
  transfers between devices with their start and end apart: 2 -> 0, of which waited for: 2 -> 0; matrix products, arithmetic and copies ran while one was open for 1% -> 0% of each run, Pallas kernels for 0% -> 0%
where the time goes in v2:
time: 103 us
  Pallas kernels  101 us (98%)
  local copies, waits for them, and re-layouts  1.57 us (2%)
    pallas_call x1, Pallas kernels, body(): pl.pallas_call(kernel, out_shape=jax.ShapeDtypeStruct((feat, nodes), jnp....  101 us

profile of v2, /device:TPU:2, one launch (start us, length us, event | category | flops | bytes accessed | tf_op | source)
XLA Modules:
  0.0 103.1 jit_solution(6994687476938435793)
XLA Ops:
  0.7 100.9 %shard_map.91 = f32[64,512]{1,0:T(8,128)} custom-call(s32[64]{0:T(128)} %cols_ref.1, s32[64]{0:T(128)} %rows_ref.1, s32[1]{0:T(128)S(6)} %copy.11.count_ref, bf16[64,512]{1,0:T(8,128)(2,1)} %x_ref.1, bf16[64,128,128]{2,1,0:T(8,128)(2,1)} %adj_ref.1, bf16[64,512]{1,0:T(8,128)(2,1)} %w1_ref.1, f32[1,64]{1,0:T(1,128)} %bitcast.2, bf16[64,512]{1,0:T(8,128)(2,1)} %w2_ref.1, ...), custom_call_target="tpu_custom_call" | custom-call | tf_op jit(solution)/shard_map/pallas_call | solution.py:295
  101.6 1.6 %copy.12 = f32[64,512]{1,0:T(8,128)} copy(f32[64,512]{1,0:T(8,128)} %shard_map.91) | data formatting | bytes 262144

commit v3 on v2

--- a/solution.py
+++ b/solution.py
@@ -15,44 +15,40 @@
 SIDE = 8
 FAR, NEAR = 4, 3
 HALF = 2
+CAP = 2
+WIRE, BASE, HOP = 1.0, 0.9, 0.8
 SLOTS = 64
 
 
-def children(flow, at):
-    first, second = (0, 1) if flow == 0 else (1, 0)
-    out = []
-
-    def step(axis):
-        here = at[axis]
-        for sign in (1, -1):
-            if (sign > 0 and 0 <= here < FAR) or (sign < 0 and -NEAR < here <= 0):
-                there = list(at)
-                there[axis] += sign
-                out.append((tuple(there), axis, sign))
-
-    if at[second] == 0:
-        step(first)
-    step(second)
+SPINES = (0, 3, -3)
+BESIDE = {0: (1, -1), 3: (1, -1), -3: (1,)}
+
+
+def onward(at):
+    a, b = at
+    out = [(d, 0) for d in SPINES if d] if at == (0, 0) else []
+    if 0 <= b < FAR:
+        out.append((a, b + 1))
+    if -NEAR < b <= 0:
+        out.append((a, b - 1))
     return out
 
 
-def depth(flow, at):
-    return max([1 + depth(flow, there) for there, _, _ in children(flow, at)], default=0)
-
-
 def arrival_order():
-    wire, hop = 0.7, 1.7
+    wire, base, hop = WIRE, BASE, HOP
     free = {}
     tick = itertools.count()
-    events = [(0.0, next(tick), flow, (0, 0)) for flow in (0, 1)]
+    events = [(0.0, next(tick), (0, 0))]
     order = []
     while events:
-        now, _, flow, at = heapq.heappop(events)
-        order.append((flow, at))
-        for there, axis, sign in sorted(children(flow, at), key=lambda c: -depth(flow, c[0])):
-            start = max(now, free.get((axis, sign), 0.0))
-            free[(axis, sign)] = start + wire
-            heapq.heappush(events, (free[(axis, sign)] + hop, next(tick), flow, there))
+        now, _, at = heapq.heappop(events)
+        order.append(at)
+        for there in onward(at):
+            da, db = there[0] - at[0], there[1] - at[1]
+            link = (da != 0, da + db > 0)
+            start = max(now, free.get(link, 0.0))
+            free[link] = start + wire * abs(da + db)
+            heapq.heappush(events, (start + wire + base + hop * abs(da + db), next(tick), there))
     return order
 
 
@@ -63,18 +59,19 @@
 class Place:
     def __init__(self):
         self.node, self.col = lax.axis_index("node"), lax.axis_index("col")
-        self.y, self.z = self.node // SIDE, self.node % SIDE
+        y, z = self.node // SIDE, self.node % SIDE
         self.x, self.core = self.col // 2, self.col % 2
-        self.sign = 1 - 2 * self.core
-        self.ys = {a: (self.y - self.sign * a + 2 * SIDE) % SIDE for a in range(-NEAR, FAR + 1)}
-        self.zs = {a: (self.z - self.sign * a + 2 * SIDE) % SIDE for a in range(-NEAR, FAR + 1)}
+        self.u, v = y + (z - y) * self.core, z + (y - z) * self.core
+        across, along = SIDE - (SIDE - 1) * self.core, 1 + (SIDE - 1) * self.core
+        steps = range(-FAR, FAR + 1)
+        self.us = {a: (self.u + a + SIDE) % SIDE * across for a in steps}
+        self.vs = {b: (v - b + SIDE) % SIDE * along for b in steps}
 
     def source(self, at):
-        return self.ys[at[0]] * SIDE + self.zs[at[1]]
-
-    def toward(self, axis, sign):
-        y, z = (self.ys[-sign], self.z) if axis == 0 else (self.y, self.zs[-sign])
-        return (y * SIDE + z, self.col)
+        return self.us[at[0]] + self.vs[at[1]]
+
+    def target(self, da, db):
+        return (self.us[-da] + self.vs[-db], self.col)
 
     def beside(self, dx, other):
         core = 1 - self.core if other else self.core
@@ -87,31 +84,46 @@
     )
 
 
-def node_gather(place, held, send, recv, ends, own, between=None):
+def node_gather(place, held, stage, table, send, recv, ends, between=None):
     here = (place.node, place.col)
-    last = 0
-    for count, (flow, at) in enumerate(arrival_order()):
-        rows = held.at[pl.ds(place.source(at) * RB + flow * HALF, HALF)]
-        onward = sorted(children(flow, at), key=lambda c: -depth(flow, c[0]))
+    picked, ready = 0, []
+
+    def pick(at):
+        nonlocal picked
+        base = place.source(at) * RB
+        blocks = [held[base + k] for k in range(RB)]
+        copies = []
+        for da in BESIDE[at[0]]:
+            for lane in range(CAP):
+                want = table[(1 - da) // 2, place.source(at), lane]
+                block = blocks[RB - 1]
+                for k in range(RB - 1):
+                    block = jnp.where(want == k, blocks[k], block)
+                stage[picked, lane] = block
+            pair = held.at[pl.ds(base, CAP)]
+            copies.append(remote(stage.at[picked], pair, send, ends, place.target(da, 0)))
+            picked += 1
+        return copies
+
+    order = arrival_order()
+    for count, at in enumerate(order):
+        rows = held.at[pl.ds(place.source(at) * RB, RB)]
         if at != (0, 0):
-            if not onward:
-                last += 1
-                continue
-            remote(rows, rows, send, recv.at[flow * SLOTS + slot_of(at)], here).wait_recv()
-        for there, axis, sign in onward:
-            ending = not children(flow, there)
-            sem = ends if ending else recv.at[flow * SLOTS + slot_of(there)]
-            device = place.toward(axis, sign)
-            if at == (0, 0) and own is not None:
-                for k in range(flow * HALF, flow * HALF + HALF):
-                    remote(own(k), held.at[place.node * RB + k], send, sem, device).start()
-            else:
-                remote(rows, rows, send, sem, device).start()
+            remote(rows, rows, send, recv.at[slot_of(at)], here).wait_recv()
+        for there in onward(at):
+            remote(rows, rows, send, recv.at[slot_of(there)], place.target(there[0] - at[0], there[1] - at[1])).start()
         if between is not None:
             between(count)
-    whole = held.at[pl.ds(0, last * HALF)]
-    remote(whole, whole, send, ends, here).wait_recv()
-    sent = held.at[pl.ds(0, (SIDE * SIDE - 1) * RB)]
+        for copy in ready:
+            copy.start()
+        ready = pick(order[count - 1]) if count else []
+    for copy in ready:
+        copy.start()
+    for copy in pick(order[-1]):
+        copy.start()
+    came = held.at[pl.ds(0, picked * CAP)]
+    remote(came, came, send, ends, here).wait_recv()
+    sent = held.at[pl.ds(0, (len(order) - 1) * RB + picked * CAP)]
     remote(sent, sent, send, ends, here).wait_send()
 
 
@@ -173,7 +185,7 @@
         left, right = [], []
         for k in range(GROUP):
             t = g * GROUP + k
-            block = gathered[index_ref[t]]
+            block = gathered[index_ref[0, t]]
             row = jnp.where(t < live, rows_ref[t], RB)
             zero = jnp.zeros_like(block)
             left.append(jnp.concatenate([jnp.where(row == b, block, zero) for b in range(RB)], axis=0))
@@ -195,10 +207,28 @@
     return jnp.sum(jnp.where(same, square, 0.0), axis=1, keepdims=True)
 
 
+def tile_plan(place, cols, live):
+    total, nodes = cols.shape[1], SIDE * SIDE
+    node, block = cols >> 2, cols & (RB - 1)
+    alive = lax.broadcasted_iota(jnp.int32, (1, total), 1) < live
+    node = jnp.where(alive, node, nodes)
+    hit = lax.broadcasted_iota(jnp.int32, (nodes, total), 0) == node
+    first = jnp.min(jnp.where(hit, block, RB - 1).astype(jnp.float32), axis=1, keepdims=True).astype(jnp.int32)
+    last = jnp.max(jnp.where(hit, block, 0).astype(jnp.float32), axis=1, keepdims=True).astype(jnp.int32)
+    lowest = jnp.min(jnp.where(hit, first, RB - 1).astype(jnp.float32), axis=0, keepdims=True).astype(jnp.int32)
+    owner = cols >> 2
+    u = (owner >> 3) * (1 - place.core) + (owner & (SIDE - 1)) * place.core
+    a = (u - place.u + SIDE) & (SIDE - 1)
+    line = (a == 0) | (a == 3) | (a == SIDE - 3)
+    slot = jnp.where(line, block, jnp.where(block == lowest, 0, 1))
+    return first, last, owner * RB + slot
+
+
 def kernel(
-    cols_ref, rows_ref, count_ref, x_ref, adj_ref, w1_ref, b1_ref, w2_ref, b2_ref, out_ref,
+    colrow_ref, rows_ref, count_ref, x_ref, adj_ref, w1_ref, b1_ref, w2_ref, b2_ref, out_ref,
     held1, held2, tiles, w1_all, w2, b1_own, b1_all, y_own, y_all,
-    recv1, recv2, col_recv, bias_recv, sends, local,
+    stage, wanted, wanted_by, index_row, table, index_ref,
+    recv1, recv2, col_recv, bias_recv, want_recv, sends, local,
 ):
     feat = y_own.shape[0]
     place = Place()
@@ -214,13 +244,26 @@
 
     b1_own[...] = jnp.broadcast_to(as_column(b1_ref[...]), b1_own.shape)
     b1_all[pl.ds(place.col * feat, feat)] = b1_own[...]
+    first, last, index = tile_plan(place, colrow_ref[...], count_ref[0])
+    lane = lax.broadcasted_iota(jnp.int32, wanted.shape, 1)
+    wanted[...] = jnp.where(lane == 0, first, last)
+    index_row[:, 0 : index.shape[1]] = jnp.broadcast_to(index, (8, index.shape[1]))
+    for copy in fetch[3:]:
+        copy.wait()
 
     barrier = pltpu.get_barrier_semaphore()
-    greeted = [place.toward(axis, sign) for axis in (0, 1) for sign in (1, -1)]
+    greeted = [place.target(d, 0) for d in (1, -1, 3, -3)] + [place.target(0, d) for d in (1, -1)]
     greeted += [place.beside(dx, other) for dx in range(4) for other in (False, True) if dx or other]
     for device in greeted:
         pl.semaphore_signal(barrier, inc=1, device_id=device, device_id_type=MESH)
     pl.semaphore_wait(barrier, len(greeted))
+
+    asked = [remote(wanted, wanted_by.at[i], sends.at[5 + i], want_recv.at[i], place.target(d, 0)) for i, d in ((1, 1), (0, -1))]
+    for copy in asked:
+        copy.start()
+    to_index = pltpu.make_async_copy(index_row, index_ref, local.at[7])
+    to_index.start()
+    to_table = pltpu.make_async_copy(wanted_by, table, local.at[8])
 
     weights = ColGather(place, w1_ref, w1_all, feat, sends.at[2], col_recv.at[0])
     peers = [(dx, other) for dx in range(4) for other in (False, True) if dx or other]
@@ -234,25 +277,30 @@
 
     def between(count):
         if count == 1:
+            for copy in asked:
+                copy.wait()
+            to_table.start()
             weights.begin()
             for index, (dx, other) in enumerate(peers):
                 bias_copy(index, dx, other, False).start()
-        elif count == 20:
+            to_table.wait()
+        elif count == 8:
             weights.forward(0)
-        elif count == 40:
+        elif count == 16:
             weights.forward(1)
 
-    node_gather(place, held1, sends.at[0], recv1, recv1.at[2 * SLOTS], lambda k: x_ref.at[:, pl.ds(k * BLK, BLK)], between)
+    node_gather(place, held1, stage, table, sends.at[0], recv1, recv1.at[SLOTS], between)
+    to_index.wait()
     weights.finish()
     for index, (dx, other) in enumerate(peers):
         bias_copy(index, dx, other, True).wait_recv()
     sent = b1_all.at[pl.ds(0, len(peers) * feat)]
     remote(sent, sent, sends.at[4], bias_recv.at[0], (place.node, place.col)).wait_send()
-    for copy in fetch:
+    for copy in fetch[:3]:
         copy.wait()
 
     live = count_ref[0]
-    acc = tile_sum(cols_ref, rows_ref, live, held1, tiles)
+    acc = tile_sum(index_ref, rows_ref, live, held1, tiles)
     for b in range(RB):
         y_own[:, b * BLK : (b + 1) * BLK] = acc[b * feat : (b + 1) * feat].astype(y_own.dtype)
     y_all[pl.ds(place.col * feat, feat)] = y_own[...]
@@ -276,8 +324,8 @@
         for k in range(HALF):
             held2[place.node * RB + n * HALF + k] = total[:, k * BLK : (k + 1) * BLK].astype(jnp.bfloat16)
 
-    node_gather(place, held2, sends.at[1], recv2, recv2.at[2 * SLOTS], None)
-    acc = tile_sum(cols_ref, rows_ref, live, held2, tiles)
+    node_gather(place, held2, stage, table, sends.at[1], recv2, recv2.at[SLOTS])
+    acc = tile_sum(index_ref, rows_ref, live, held2, tiles)
     bias = as_column(b2_ref[...])
     for b in range(RB):
         out_ref[:, b * BLK : (b + 1) * BLK] = acc[b * feat : (b + 1) * feat] + bias
@@ -295,7 +343,7 @@
     return pl.pallas_call(
         kernel,
         out_shape=jax.ShapeDtypeStruct((feat, nodes), jnp.float32),
-        in_specs=[smem, smem, smem, hbm, hbm, hbm, vmem, hbm, vmem],
+        in_specs=[vmem, smem, smem, hbm, hbm, hbm, vmem, hbm, vmem],
         out_specs=vmem,
         scratch_shapes=[
             pltpu.VMEM((blocks, feat, BLK), bf16),
@@ -307,15 +355,22 @@
             pltpu.VMEM((channels, BLK), jnp.float32),
             pltpu.VMEM((feat, nodes), bf16),
             pltpu.VMEM((channels, nodes), bf16),
-            dma((2 * SLOTS + 1,)),
-            dma((2 * SLOTS + 1,)),
+            pltpu.VMEM((5 * SIDE, CAP, feat, BLK), bf16),
+            pltpu.VMEM((SIDE * SIDE, BLK), jnp.int32),
+            pltpu.VMEM((2, SIDE * SIDE, BLK), jnp.int32),
+            pltpu.VMEM((8, BLK), jnp.int32),
+            pltpu.SMEM((2, SIDE * SIDE, BLK), jnp.int32),
+            pltpu.SMEM((8, BLK), jnp.int32),
+            dma((SLOTS + 1,)),
+            dma((SLOTS + 1,)),
             dma((2, 13)),
             dma((7,)),
-            dma((5,)),
+            dma((2,)),
             dma((7,)),
+            dma((9,)),
         ],
         compiler_params=pltpu.CompilerParams(collective_id=0, has_side_effects=True),
-    )(tile_cols, tile_rows, tile_counts, x_t, adj_tiles, w_first, b_first[None, :], w_second, b_second[None, :])
+    )(tile_cols[None, :], tile_rows, tile_counts, x_t, adj_tiles, w_first, b_first[None, :], w_second, b_second[None, :])
 
 
 def solution(mesh):

time: 103 us -> 90.4 us (0.88)
  Pallas kernels: 101 us -> 88 us
    pallas_call x1, Pallas kernels: 101 us -> 88 us  [body(): pl.pallas_call(kernel, out_shape=jax.ShapeDtypeStruct((feat, nodes), jnp....]
where the time goes in v3:
time: 90.4 us; the launch traced here: 90.2 us
  Pallas kernels  88 us (97%)
  local copies, waits for them, and re-layouts  1.57 us (2%)
    pallas_call x1, Pallas kernels, body(): pl.pallas_call(kernel, out_shape=jax.ShapeDtypeStruct((feat, nodes), jnp....  88 us

profile of v3, /device:TPU:2, one launch (start us, length us, event | category | flops | bytes accessed | tf_op | source)
XLA Modules:
  0.0 90.2 jit_solution(6895213655292158163)
XLA Ops:
  0.7 88.0 %shard_map.91 = f32[64,512]{1,0:T(8,128)} custom-call(s32[1,64]{1,0:T(1,128)} %bitcast.3, s32[64]{0:T(128)} %rows_ref.1, s32[1]{0:T(128)S(6)} %copy.11.count_ref, bf16[64,512]{1,0:T(8,128)(2,1)} %x_ref.1, bf16[64,128,128]{2,1,0:T(8,128)(2,1)} %adj_ref.1, bf16[64,512]{1,0:T(8,128)(2,1)} %w1_ref.1, f32[1,64]{1,0:T(1,128)} %bitcast.4, bf16[64,512]{1,0:T(8,128)(2,1)} %w2_ref.1, ...), custom_call_target="tpu_custom_call" | custom-call | tf_op jit(solution)/shard_map/pallas_call | solution.py:343
  88.6 1.6 %copy.12 = f32[64,512]{1,0:T(8,128)} copy(f32[64,512]{1,0:T(8,128)} %shard_map.91) | data formatting | bytes 262144

commit v4 on v3

--- a/solution.py
+++ b/solution.py
@@ -11,27 +11,31 @@
 MESH = pl.DeviceIdType.MESH
 BLK = 128
 RB = 4
-GROUP = 8
+GROUP = 32
 SIDE = 8
 FAR, NEAR = 4, 3
 HALF = 2
 CAP = 2
-WIRE, BASE, HOP = 1.0, 0.9, 0.8
+WIRE, BASE, HOP = 0.6, 0.9, 0.5
+TABLE = 2
 SLOTS = 64
 
 
 SPINES = (0, 3, -3)
 BESIDE = {0: (1, -1), 3: (1, -1), -3: (1,)}
+ROWS = (1, -1, 2, 4, -2)
+SPANS = ((-1, 0), (1, 2), (-2, -2), (-3, -3), (3, 3), (4, 4))
+FULL = SIDE * SIDE * RB
 
 
 def onward(at):
     a, b = at
-    out = [(d, 0) for d in SPINES if d] if at == (0, 0) else []
+    out = []
     if 0 <= b < FAR:
         out.append((a, b + 1))
     if -NEAR < b <= 0:
         out.append((a, b - 1))
-    return out
+    return out + ([(d, 0) for d in SPINES if d] if at == (0, 0) else [])
 
 
 def arrival_order():
@@ -61,11 +65,11 @@
         self.node, self.col = lax.axis_index("node"), lax.axis_index("col")
         y, z = self.node // SIDE, self.node % SIDE
         self.x, self.core = self.col // 2, self.col % 2
-        self.u, v = y + (z - y) * self.core, z + (y - z) * self.core
+        self.u, self.v = y + (z - y) * self.core, z + (y - z) * self.core
         across, along = SIDE - (SIDE - 1) * self.core, 1 + (SIDE - 1) * self.core
         steps = range(-FAR, FAR + 1)
         self.us = {a: (self.u + a + SIDE) % SIDE * across for a in steps}
-        self.vs = {b: (v - b + SIDE) % SIDE * along for b in steps}
+        self.vs = {b: (self.v - b + SIDE) % SIDE * along for b in steps}
 
     def source(self, at):
         return self.us[at[0]] + self.vs[at[1]]
@@ -84,25 +88,33 @@
     )
 
 
-def node_gather(place, held, stage, table, send, recv, ends, between=None):
+def pair_at(a, b):
+    return (ROWS.index(a) * SIDE + b + NEAR) * CAP
+
+
+def node_gather(place, held, stage, table, send, recv, ends, start=1, between=None):
     here = (place.node, place.col)
-    picked, ready = 0, []
+    picked = set()
+    waiting = []
 
     def pick(at):
-        nonlocal picked
+        a, b = at
         base = place.source(at) * RB
         blocks = [held[base + k] for k in range(RB)]
+        picked.add(at)
         copies = []
-        for da in BESIDE[at[0]]:
+        low, high = next(span for span in SPANS if span[0] <= b <= span[1])
+        for da in BESIDE[a]:
             for lane in range(CAP):
                 want = table[(1 - da) // 2, place.source(at), lane]
                 block = blocks[RB - 1]
                 for k in range(RB - 1):
                     block = jnp.where(want == k, blocks[k], block)
-                stage[picked, lane] = block
-            pair = held.at[pl.ds(base, CAP)]
-            copies.append(remote(stage.at[picked], pair, send, ends, place.target(da, 0)))
-            picked += 1
+                stage[pair_at(a + da, b) + lane] = block
+            if all((a, other) in picked for other in range(low, high + 1)):
+                first, size = pair_at(a + da, low), CAP * (high + 1 - low)
+                pairs = held.at[pl.ds(FULL + first, size)]
+                copies.append(remote(stage.at[pl.ds(first, size)], pairs, send, ends, place.target(da, 0)))
         return copies
 
     order = arrival_order()
@@ -114,16 +126,19 @@
             remote(rows, rows, send, recv.at[slot_of(there)], place.target(there[0] - at[0], there[1] - at[1])).start()
         if between is not None:
             between(count)
-        for copy in ready:
+        if count >= start:
+            for old in waiting + [at]:
+                for copy in pick(old):
+                    copy.start()
+            waiting = []
+        else:
+            waiting.append(at)
+    for at in waiting:
+        for copy in pick(at):
             copy.start()
-        ready = pick(order[count - 1]) if count else []
-    for copy in ready:
-        copy.start()
-    for copy in pick(order[-1]):
-        copy.start()
-    came = held.at[pl.ds(0, picked * CAP)]
+    came = held.at[pl.ds(0, len(ROWS) * SIDE * CAP)]
     remote(came, came, send, ends, here).wait_recv()
-    sent = held.at[pl.ds(0, (len(order) - 1) * RB + picked * CAP)]
+    sent = held.at[pl.ds(0, (len(order) - 1) * RB + len(ROWS) * SIDE * CAP)]
     remote(sent, sent, send, ends, here).wait_send()
 
 
@@ -145,34 +160,26 @@
 
     def begin(self):
         p = self.place
-        for dx, part, sem in ((1, 0, 0), (-1, 1, 3), (1, 1, 1), (-1, 0, 2)):
-            remote(self.mine(part), self.cut(p.x, p.core, part), self.send, self.recv.at[sem], p.beside(dx + 4, False)).start()
-        remote(self.mine(None), self.cut(p.x, p.core, None), self.send, self.recv.at[4], p.beside(0, True)).start()
-
-    def wait(self, dx, other, part, sem):
+        for dx, sem in ((1, 0), (-1, 1), (2, 2)):
+            remote(self.own, self.cut(p.x, p.core, None), self.send, self.recv.at[sem], p.beside(dx + 4, False)).start()
+        remote(self.own, self.cut(p.x, p.core, None), self.send, self.recv.at[3], p.beside(0, True)).start()
+
+    def wait(self, dx, other, sem):
         p = self.place
         core = 1 - p.core if other else p.core
-        rows = self.cut(p.x + dx + 4, core, part)
+        rows = self.cut(p.x + dx + 4, core, None)
         remote(rows, rows, self.send, self.recv.at[sem], (p.node, p.col)).wait_recv()
         return rows
 
     def forward(self, stage):
         p = self.place
-        if stage == 0:
-            for dx, part, sem, on, far in ((-1, 0, 0, 1, 5), (1, 1, 3, -1, 6), (-1, 1, 1, 0, 0), (1, 0, 2, 0, 0)):
-                rows = self.wait(dx, False, part, sem)
-                if on:
-                    remote(rows, rows, self.send, self.recv.at[far], p.beside(on + 4, False)).start()
-                remote(rows, rows, self.send, self.recv.at[7 + sem], p.beside(0, True)).start()
-        else:
-            for part, sem in ((0, 5), (1, 6)):
-                rows = self.wait(2, False, part, sem)
-                remote(rows, rows, self.send, self.recv.at[6 + sem], p.beside(0, True)).start()
+        for dx, sem in ((-1, 0), (1, 1)) if stage == 0 else ((2, 2),):
+            rows = self.wait(dx, False, sem)
+            remote(rows, rows, self.send, self.recv.at[4 + sem], p.beside(0, True)).start()
 
     def finish(self):
-        self.wait(0, True, None, 4)
-        for dx, part, sem in ((-1, 0, 7), (-1, 1, 8), (1, 0, 9), (1, 1, 10), (2, 0, 11), (2, 1, 12)):
-            self.wait(dx, True, part, sem)
+        for dx, sem in ((0, 3), (-1, 4), (1, 5), (2, 6)):
+            self.wait(dx, True, sem)
         sent = self.rows.at[pl.ds(0, 7 * self.feat)]
         remote(sent, sent, self.send, self.recv.at[0], (self.place.node, self.place.col)).wait_send()
 
@@ -220,8 +227,13 @@
     u = (owner >> 3) * (1 - place.core) + (owner & (SIDE - 1)) * place.core
     a = (u - place.u + SIDE) & (SIDE - 1)
     line = (a == 0) | (a == 3) | (a == SIDE - 3)
-    slot = jnp.where(line, block, jnp.where(block == lowest, 0, 1))
-    return first, last, owner * RB + slot
+    v = (owner & (SIDE - 1)) * (1 - place.core) + (owner >> 3) * place.core
+    row = jnp.zeros_like(a)
+    for i, at in enumerate(ROWS):
+        row = jnp.where(a == at % SIDE, i, row)
+    pair = (row * SIDE + ((place.v - v + NEAR) & (SIDE - 1))) * CAP
+    beside = FULL + pair + jnp.where(block == lowest, 0, 1)
+    return first, last, jnp.where(line, owner * RB + block, beside)
 
 
 def kernel(
@@ -233,36 +245,27 @@
     feat = y_own.shape[0]
     place = Place()
     fetch = [
-        pltpu.make_async_copy(adj_ref, tiles, local.at[0]),
-        pltpu.make_async_copy(w2_ref, w2, local.at[1]),
-        pltpu.make_async_copy(w1_ref, w1_all.at[pl.ds(place.col * feat, feat)], local.at[2]),
+        pltpu.make_async_copy(x_ref.at[:, pl.ds(k * BLK, BLK)], held1.at[place.node * RB + k], local.at[k]) for k in range(RB)
     ]
-    for k in range(RB):
-        fetch.append(pltpu.make_async_copy(x_ref.at[:, pl.ds(k * BLK, BLK)], held1.at[place.node * RB + k], local.at[3 + k]))
+    fetch += [
+        pltpu.make_async_copy(adj_ref, tiles, local.at[4]),
+        pltpu.make_async_copy(w2_ref, w2, local.at[5]),
+        pltpu.make_async_copy(w1_ref, w1_all.at[pl.ds(place.col * feat, feat)], local.at[6]),
+    ]
     for copy in fetch:
         copy.start()
-
-    b1_own[...] = jnp.broadcast_to(as_column(b1_ref[...]), b1_own.shape)
-    b1_all[pl.ds(place.col * feat, feat)] = b1_own[...]
-    first, last, index = tile_plan(place, colrow_ref[...], count_ref[0])
-    lane = lax.broadcasted_iota(jnp.int32, wanted.shape, 1)
-    wanted[...] = jnp.where(lane == 0, first, last)
-    index_row[:, 0 : index.shape[1]] = jnp.broadcast_to(index, (8, index.shape[1]))
-    for copy in fetch[3:]:
-        copy.wait()
 
     barrier = pltpu.get_barrier_semaphore()
     greeted = [place.target(d, 0) for d in (1, -1, 3, -3)] + [place.target(0, d) for d in (1, -1)]
     greeted += [place.beside(dx, other) for dx in range(4) for other in (False, True) if dx or other]
     for device in greeted:
         pl.semaphore_signal(barrier, inc=1, device_id=device, device_id_type=MESH)
+    for copy in fetch[:RB]:
+        copy.wait()
     pl.semaphore_wait(barrier, len(greeted))
 
     asked = [remote(wanted, wanted_by.at[i], sends.at[5 + i], want_recv.at[i], place.target(d, 0)) for i, d in ((1, 1), (0, -1))]
-    for copy in asked:
-        copy.start()
     to_index = pltpu.make_async_copy(index_row, index_ref, local.at[7])
-    to_index.start()
     to_table = pltpu.make_async_copy(wanted_by, table, local.at[8])
 
     weights = ColGather(place, w1_ref, w1_all, feat, sends.at[2], col_recv.at[0])
@@ -276,27 +279,38 @@
         return remote(b1_own, rows, sends.at[4], bias_recv.at[index], place.beside(dx, other))
 
     def between(count):
-        if count == 1:
+        if count == 0:
+            weights.begin()
+            first, last, index = tile_plan(place, colrow_ref[...], count_ref[0])
+            lane = lax.broadcasted_iota(jnp.int32, wanted.shape, 1)
+            wanted[...] = jnp.where(lane == 0, first, last)
+            index_row[:, 0 : index.shape[1]] = jnp.broadcast_to(index, (8, index.shape[1]))
+            b1_own[...] = jnp.broadcast_to(as_column(b1_ref[...]), b1_own.shape)
+            b1_all[pl.ds(place.col * feat, feat)] = b1_own[...]
+            for copy in asked:
+                copy.start()
+            to_index.start()
+            for index, (dx, other) in enumerate(peers):
+                bias_copy(index, dx, other, False).start()
+        elif count == TABLE:
             for copy in asked:
                 copy.wait()
             to_table.start()
-            weights.begin()
-            for index, (dx, other) in enumerate(peers):
-                bias_copy(index, dx, other, False).start()
+        elif count == TABLE + 1:
             to_table.wait()
-        elif count == 8:
+        elif count == TABLE + 5:
             weights.forward(0)
-        elif count == 16:
+        elif count == TABLE + 12:
             weights.forward(1)
 
-    node_gather(place, held1, stage, table, sends.at[0], recv1, recv1.at[SLOTS], between)
+    node_gather(place, held1, stage, table, sends.at[0], recv1, recv1.at[SLOTS], TABLE + 1, between)
     to_index.wait()
     weights.finish()
     for index, (dx, other) in enumerate(peers):
         bias_copy(index, dx, other, True).wait_recv()
     sent = b1_all.at[pl.ds(0, len(peers) * feat)]
     remote(sent, sent, sends.at[4], bias_recv.at[0], (place.node, place.col)).wait_send()
-    for copy in fetch[:3]:
+    for copy in fetch[RB:]:
         copy.wait()
 
     live = count_ref[0]
@@ -334,7 +348,7 @@
 def body(x_t, adj_tiles, tile_rows, tile_cols, tile_counts, w_first, b_first, w_second, b_second):
     feat, nodes = x_t.shape
     channels = w_first.shape[1]
-    blocks = SIDE * SIDE * RB
+    pairs = len(ROWS) * SIDE * CAP
     smem = pl.BlockSpec(memory_space=pltpu.SMEM)
     vmem = pl.BlockSpec(memory_space=pltpu.VMEM)
     hbm = pl.BlockSpec(memory_space=pl.ANY)
@@ -346,8 +360,8 @@
         in_specs=[vmem, smem, smem, hbm, hbm, hbm, vmem, hbm, vmem],
         out_specs=vmem,
         scratch_shapes=[
-            pltpu.VMEM((blocks, feat, BLK), bf16),
-            pltpu.VMEM((blocks, feat, BLK), bf16),
+            pltpu.VMEM((FULL + pairs, feat, BLK), bf16),
+            pltpu.VMEM((FULL + pairs, feat, BLK), bf16),
             pltpu.VMEM(adj_tiles.shape, bf16),
             pltpu.VMEM((channels, channels), bf16),
             pltpu.VMEM((feat, channels), bf16),
@@ -355,7 +369,7 @@
             pltpu.VMEM((channels, BLK), jnp.float32),
             pltpu.VMEM((feat, nodes), bf16),
             pltpu.VMEM((channels, nodes), bf16),
-            pltpu.VMEM((5 * SIDE, CAP, feat, BLK), bf16),
+            pltpu.VMEM((pairs, feat, BLK), bf16),
             pltpu.VMEM((SIDE * SIDE, BLK), jnp.int32),
             pltpu.VMEM((2, SIDE * SIDE, BLK), jnp.int32),
             pltpu.VMEM((8, BLK), jnp.int32),
@@ -363,7 +377,7 @@
             pltpu.SMEM((8, BLK), jnp.int32),
             dma((SLOTS + 1,)),
             dma((SLOTS + 1,)),
-            dma((2, 13)),
+            dma((2, 7)),
             dma((7,)),
             dma((2,)),
             dma((7,)),

time: 90.4 us -> 80.2 us (0.89)
  the two profiles are of different devices: /device:TPU:2 before, /device:TPU:8 now
where the time goes in v4:
time: 80.2 us; the launch traced here: 80.1 us
  Pallas kernels  77.8 us (97%)
  local copies, waits for them, and re-layouts  1.57 us (2%)
    pallas_call x1, Pallas kernels, body(): pl.pallas_call(kernel, out_shape=jax.ShapeDtypeStruct((feat, nodes), jnp....  77.8 us

profile of v4, /device:TPU:8, one launch (start us, length us, event | category | flops | bytes accessed | tf_op | source)
XLA Modules:
  0.0 80.1 jit_solution(14142700264958020888)
XLA Ops:
  0.7 77.8 %shard_map.91 = f32[64,512]{1,0:T(8,128)} custom-call(s32[1,64]{1,0:T(1,128)} %bitcast.3, s32[64]{0:T(128)} %rows_ref.1, s32[1]{0:T(128)S(6)} %copy.11.count_ref, bf16[64,512]{1,0:T(8,128)(2,1)} %x_ref.1, bf16[64,128,128]{2,1,0:T(8,128)(2,1)} %adj_ref.1, bf16[64,512]{1,0:T(8,128)(2,1)} %w1_ref.1, f32[1,64]{1,0:T(1,128)} %bitcast.4, bf16[64,512]{1,0:T(8,128)(2,1)} %w2_ref.1, ...), custom_call_target="tpu_custom_call" | custom-call | tf_op jit(solution)/shard_map/pallas_call | solution.py:357
  78.5 1.6 %copy.12 = f32[64,512]{1,0:T(8,128)} copy(f32[64,512]{1,0:T(8,128)} %shard_map.91) | data formatting | bytes 262144

commit v5 on v4

--- a/solution.py
+++ b/solution.py
@@ -18,6 +18,7 @@
 CAP = 2
 WIRE, BASE, HOP = 0.6, 0.9, 0.5
 TABLE = 2
+PARTS = 2
 SLOTS = 64
 
 
@@ -31,7 +32,9 @@
 def onward(at):
     a, b = at
     out = []
-    if 0 <= b < FAR:
+    if b == 2 and a:
+        out += [(a, 4), (a, 3)]
+    elif 0 <= b < FAR and not (b == 3 and a):
         out.append((a, b + 1))
     if -NEAR < b <= 0:
         out.append((a, b - 1))
@@ -143,14 +146,14 @@
 
 
 class ColGather:
-    def __init__(self, place, own, rows, feat, send, recv):
+    def __init__(self, place, own, rows, feat, send, recv, shift=0):
         self.place, self.own, self.rows, self.feat, self.send, self.recv = place, own, rows, feat, send, recv
-        self.half = feat // 2
+        self.shift, self.size = shift, own.shape[0]
 
     def cut(self, x, core, part):
         start = (x % 4 * 2 + core) * self.feat
         if part is None:
-            return self.rows.at[pl.ds(start, self.feat)]
+            return self.rows.at[pl.ds(start + self.shift, self.size)]
         return self.rows.at[pl.ds(start + part * self.half, self.half)]
 
     def mine(self, part):
@@ -180,19 +183,18 @@
     def finish(self):
         for dx, sem in ((0, 3), (-1, 4), (1, 5), (2, 6)):
             self.wait(dx, True, sem)
-        sent = self.rows.at[pl.ds(0, 7 * self.feat)]
+        sent = self.rows.at[pl.ds(0, 7 * self.size)]
         remote(sent, sent, self.send, self.recv.at[0], (self.place.node, self.place.col)).wait_send()
 
 
-def tile_sum(index_ref, rows_ref, live, gathered, tiles):
-    feat = gathered.shape[1]
+def tile_sum(index_ref, rows_ref, live, gathered, tiles, low, feat):
     total = tiles.shape[0]
 
     def step(g, acc):
         left, right = [], []
         for k in range(GROUP):
             t = g * GROUP + k
-            block = gathered[index_ref[0, t]]
+            block = gathered[index_ref[0, t], low : low + feat]
             row = jnp.where(t < live, rows_ref[t], RB)
             zero = jnp.zeros_like(block)
             left.append(jnp.concatenate([jnp.where(row == b, block, zero) for b in range(RB)], axis=0))
@@ -256,7 +258,7 @@
         copy.start()
 
     barrier = pltpu.get_barrier_semaphore()
-    greeted = [place.target(d, 0) for d in (1, -1, 3, -3)] + [place.target(0, d) for d in (1, -1)]
+    greeted = [place.target(d, 0) for d in (1, -1, 3, -3)] + [place.target(0, d) for d in (1, -1, 2, -2)]
     greeted += [place.beside(dx, other) for dx in range(4) for other in (False, True) if dx or other]
     for device in greeted:
         pl.semaphore_signal(barrier, inc=1, device_id=device, device_id_type=MESH)
@@ -314,15 +316,21 @@
         copy.wait()
 
     live = count_ref[0]
-    acc = tile_sum(index_ref, rows_ref, live, held1, tiles)
-    for b in range(RB):
-        y_own[:, b * BLK : (b + 1) * BLK] = acc[b * feat : (b + 1) * feat].astype(y_own.dtype)
-    y_all[pl.ds(place.col * feat, feat)] = y_own[...]
-    exchange = ColGather(place, y_own, y_all, feat, sends.at[3], col_recv.at[1])
-    exchange.begin()
-    exchange.forward(0)
-    exchange.forward(1)
-    exchange.finish()
+    exchanges = []
+    part = feat // PARTS
+    for p in range(PARTS):
+        acc = tile_sum(index_ref, rows_ref, live, held1, tiles, p * part, part)
+        for b in range(RB):
+            y_own[p * part : (p + 1) * part, b * BLK : (b + 1) * BLK] = acc[b * part : (b + 1) * part].astype(y_own.dtype)
+        y_all[pl.ds(place.col * feat + p * part, part)] = y_own[p * part : (p + 1) * part]
+        own = y_own.at[pl.ds(p * part, part)]
+        exchanges.append(ColGather(place, own, y_all, feat, sends.at[7 + p], col_recv.at[1 + p], p * part))
+        exchanges[-1].begin()
+    for leg in (0, 1):
+        for exchange in exchanges:
+            exchange.forward(leg)
+    for exchange in exchanges:
+        exchange.finish()
 
     wide = HALF * BLK
     step_rows = 128
@@ -339,7 +347,7 @@
             held2[place.node * RB + n * HALF + k] = total[:, k * BLK : (k + 1) * BLK].astype(jnp.bfloat16)
 
     node_gather(place, held2, stage, table, sends.at[1], recv2, recv2.at[SLOTS])
-    acc = tile_sum(index_ref, rows_ref, live, held2, tiles)
+    acc = tile_sum(index_ref, rows_ref, live, held2, tiles, 0, feat)
     bias = as_column(b2_ref[...])
     for b in range(RB):
         out_ref[:, b * BLK : (b + 1) * BLK] = acc[b * feat : (b + 1) * feat] + bias
@@ -377,10 +385,10 @@
             pltpu.SMEM((8, BLK), jnp.int32),
             dma((SLOTS + 1,)),
             dma((SLOTS + 1,)),
-            dma((2, 7)),
+            dma((1 + PARTS, 7)),
             dma((7,)),
             dma((2,)),
-            dma((7,)),
+            dma((7 + PARTS,)),
             dma((9,)),
         ],
         compiler_params=pltpu.CompilerParams(collective_id=0, has_side_effects=True),

time: 80.2 us -> 79.7 us (level)
  no operation moved by 1% of the time
where the time goes in v5:
time: 79.7 us; the launch traced here: 79.5 us
  Pallas kernels  77.3 us (97%)
  local copies, waits for them, and re-layouts  1.57 us (2%)
    pallas_call x1, Pallas kernels, body(): pl.pallas_call(kernel, out_shape=jax.ShapeDtypeStruct((feat, nodes), jnp....  77.3 us

profile of v5, /device:TPU:8, one launch (start us, length us, event | category | flops | bytes accessed | tf_op | source)
XLA Modules:
  0.0 79.5 jit_solution(2100969921179904858)
XLA Ops:
  0.7 77.3 %shard_map.91 = f32[64,512]{1,0:T(8,128)} custom-call(s32[1,64]{1,0:T(1,128)} %bitcast.3, s32[64]{0:T(128)} %rows_ref.1, s32[1]{0:T(128)S(6)} %copy.11.count_ref, bf16[64,512]{1,0:T(8,128)(2,1)} %x_ref.1, bf16[64,128,128]{2,1,0:T(8,128)(2,1)} %adj_ref.1, bf16[64,512]{1,0:T(8,128)(2,1)} %w1_ref.1, f32[1,64]{1,0:T(1,128)} %bitcast.4, bf16[64,512]{1,0:T(8,128)(2,1)} %w2_ref.1, ...), custom_call_target="tpu_custom_call" | custom-call | tf_op jit(solution)/shard_map/pallas_call | solution.py:365
  78.0 1.6 %copy.12 = f32[64,512]{1,0:T(8,128)} copy(f32[64,512]{1,0:T(8,128)} %shard_map.91) | data formatting | bytes 262144

commit v6 on v5

--- a/solution.py
+++ b/solution.py
@@ -282,7 +282,6 @@
 
     def between(count):
         if count == 0:
-            weights.begin()
             first, last, index = tile_plan(place, colrow_ref[...], count_ref[0])
             lane = lax.broadcasted_iota(jnp.int32, wanted.shape, 1)
             wanted[...] = jnp.where(lane == 0, first, last)
@@ -294,6 +293,7 @@
             to_index.start()
             for index, (dx, other) in enumerate(peers):
                 bias_copy(index, dx, other, False).start()
+            weights.begin()
         elif count == TABLE:
             for copy in asked:
                 copy.wait()

time: 79.7 us -> 79.5 us (level)
  no operation moved by 1% of the time
where the time goes in v6:
time: 79.5 us; the launch traced here: 79.3 us
  Pallas kernels  77.1 us (97%)
  local copies, waits for them, and re-layouts  1.57 us (2%)
    pallas_call x1, Pallas kernels, body(): pl.pallas_call(kernel, out_shape=jax.ShapeDtypeStruct((feat, nodes), jnp....  77.1 us

profile of v6, /device:TPU:8, one launch (start us, length us, event | category | flops | bytes accessed | tf_op | source)
XLA Modules:
  0.0 79.3 jit_solution(8964351058854484158)
XLA Ops:
  0.7 77.1 %shard_map.91 = f32[64,512]{1,0:T(8,128)} custom-call(s32[1,64]{1,0:T(1,128)} %bitcast.3, s32[64]{0:T(128)} %rows_ref.1, s32[1]{0:T(128)S(6)} %copy.11.count_ref, bf16[64,512]{1,0:T(8,128)(2,1)} %x_ref.1, bf16[64,128,128]{2,1,0:T(8,128)(2,1)} %adj_ref.1, bf16[64,512]{1,0:T(8,128)(2,1)} %w1_ref.1, f32[1,64]{1,0:T(1,128)} %bitcast.4, bf16[64,512]{1,0:T(8,128)(2,1)} %w2_ref.1, ...), custom_call_target="tpu_custom_call" | custom-call | tf_op jit(solution)/shard_map/pallas_call | solution.py:365
  77.8 1.6 %copy.12 = f32[64,512]{1,0:T(8,128)} copy(f32[64,512]{1,0:T(8,128)} %shard_map.91) | data formatting | bytes 262144

commit v7 on v6

--- a/solution.py
+++ b/solution.py
@@ -163,7 +163,7 @@
 
     def begin(self):
         p = self.place
-        for dx, sem in ((1, 0), (-1, 1), (2, 2)):
+        for dx, sem in ((2, 2), (1, 0), (-1, 1)):
             remote(self.own, self.cut(p.x, p.core, None), self.send, self.recv.at[sem], p.beside(dx + 4, False)).start()
         remote(self.own, self.cut(p.x, p.core, None), self.send, self.recv.at[3], p.beside(0, True)).start()
 

time: 79.5 us -> 79.2 us (level)
  no operation moved by 1% of the time
where the time goes in v7:
time: 79.2 us; the launch traced here: 79 us
  Pallas kernels  76.8 us (97%)
  local copies, waits for them, and re-layouts  1.57 us (2%)
    pallas_call x1, Pallas kernels, body(): pl.pallas_call(kernel, out_shape=jax.ShapeDtypeStruct((feat, nodes), jnp....  76.8 us

profile of v7, /device:TPU:8, one launch (start us, length us, event | category | flops | bytes accessed | tf_op | source)
XLA Modules:
  0.0 79.0 jit_solution(13231382187826880114)
XLA Ops:
  0.7 76.8 %shard_map.91 = f32[64,512]{1,0:T(8,128)} custom-call(s32[1,64]{1,0:T(1,128)} %bitcast.3, s32[64]{0:T(128)} %rows_ref.1, s32[1]{0:T(128)S(6)} %copy.11.count_ref, bf16[64,512]{1,0:T(8,128)(2,1)} %x_ref.1, bf16[64,128,128]{2,1,0:T(8,128)(2,1)} %adj_ref.1, bf16[64,512]{1,0:T(8,128)(2,1)} %w1_ref.1, f32[1,64]{1,0:T(1,128)} %bitcast.4, bf16[64,512]{1,0:T(8,128)(2,1)} %w2_ref.1, ...), custom_call_target="tpu_custom_call" | custom-call | tf_op jit(solution)/shard_map/pallas_call | solution.py:365
  77.4 1.6 %copy.12 = f32[64,512]{1,0:T(8,128)} copy(f32[64,512]{1,0:T(8,128)} %shard_map.91) | data formatting | bytes 262144
